TPU v7x, 32 devices: a whole 2x2x4 slice. The times are simulated.
32 devices in a mesh: seq: 4 (over z_hi, core), expert: 4 (over y, x), tensor: 2 (over z_lo).
Axes of the slice: x: 2, y: 2, z: 4 (z_hi: 2, z_lo: 2; z = z_hi * 2 + z_lo), core: 2. Of those that a mesh axis runs over, the one named last changes fastest.
Arguments:
- q_rows: bfloat16 [4, 512, 4096], P('expert', 'seq', 'tensor'), may hold values from -6 to 6
- k_rows: bfloat16 [4, 512, 512], P('expert', 'seq', 'tensor'), may hold values from -6 to 6
- value_rows: bfloat16 [4, 512, 512], P('expert', 'seq', 'tensor'), may hold values from -6 to 6
- x_rows: bfloat16 [4, 512, 2048], P('expert', 'seq'), may hold values from -40 to 40
- out_weight: bfloat16 [4096, 2048], P('tensor', 'expert'), may hold values from -0.09375 to 0.09375
- norm_gain: float32 [2048], P('tensor'), may hold values from 0.1 to 1.9
- w_gate: bfloat16 [16, 2048, 768], P(('seq', 'expert'), None, 'tensor'), may hold values from -0.125 to 0.125
- w_up: bfloat16 [16, 2048, 768], P(('seq', 'expert'), None, 'tensor'), may hold values from -0.125 to 0.125
- w_down: bfloat16 [16, 768, 2048], P(('seq', 'expert'), 'tensor'), may hold values from -0.21875 to 0.21875
- expert_ids: int32 [4, 512, 8], P('expert', 'seq'), may hold values from 0 to 15, all different within a row; in each aligned block of 128 rows (0 to 127, 128 to 255, ..., all dimensions but the last counted through in order) at most 96 rows name the same one
- gate_weights: float32 [4, 512, 8], P('expert', 'seq'), may hold values from 0.02 to 0.4
Outputs:
- layer_out: bfloat16 [4, 512, 2048], P('expert', 'seq', 'tensor')
Inputs may be any that keep to these rules, and one draw needn't show every extreme that they name: `expert_ids`: in each token's row the 8 ids differ. Among the 128 tokens of one block of positions (the blocks laid session after session) no expert is named more than 96 times, a bound that some block reaches; every expert is named somewhere.
All inputs are finite; a program needn't handle non-finite values.
Results may differ from a plain program's by a relative error of at most 0.007.
Values may be sent and summed in bfloat16 or wider, within the bound.
No kernel may reach another device: no remote copies, remote signals or barrier semaphores. Data moves between devices by JAX's collectives and lax.ppermute only.
A program may use at most 128 MiB of HBM per device.

v0:
```python
import math
import jax
import jax.numpy as jnp
from jax import lax
from jax.sharding import PartitionSpec as P

HEAD_SIZE = 128
TOPK = 8


def per_device(
    q_rows,
    k_rows,
    value_rows,
    x_rows,
    out_weight,
    norm_gain,
    w_gate,
    w_up,
    w_down,
    expert_ids,
    gate_weights,
):
    rows_here = q_rows.shape[1]
    kv_heads = k_rows.shape[2] // HEAD_SIZE
    q_heads = q_rows.shape[2] // HEAD_SIZE
    group_width = q_heads // kv_heads
    queries = q_rows[0].reshape(rows_here, kv_heads, group_width, HEAD_SIZE)
    offset = lax.axis_index("seq") * rows_here
    query_pos = offset + jnp.arange(rows_here, dtype=jnp.int32)
    softmax_scale = 1.0 / math.sqrt(HEAD_SIZE)
    tensor_pos = lax.axis_index("tensor")
    tensor_count = lax.axis_size("tensor")
    pieces = (
        lax.all_gather(k_rows, "seq", axis=1, tiled=True),
        lax.all_gather(value_rows, "seq", axis=1, tiled=True),
    )
    running_max = jnp.full((kv_heads, group_width, rows_here), -1e30, jnp.float32)
    block_rows = pieces[0].shape[1]
    key_block = pieces[0][0].reshape(block_rows, kv_heads, HEAD_SIZE)
    value_block = pieces[1][0].reshape(block_rows, kv_heads, HEAD_SIZE)
    scores = (
        jnp.einsum("igrd,jgd->grij", queries, key_block, preferred_element_type=jnp.float32)
        * softmax_scale
    )
    key_pos = jnp.arange(block_rows, dtype=jnp.int32)
    allowed = key_pos[None, :] <= query_pos[:, None]
    scores = jnp.where(allowed, scores, jnp.float32(-1e30))
    new_max = jnp.maximum(running_max, jnp.max(scores, axis=-1))
    weights = jnp.where(allowed, jnp.exp(scores - new_max[..., None]), jnp.float32(0.0))
    running_sum = jnp.sum(weights, axis=-1)
    weighted = jnp.einsum(
        "grij,jgd->grid",
        weights.astype(jnp.bfloat16),
        value_block,
        preferred_element_type=jnp.float32,
    )
    running_max, running_sum, weighted = (new_max, running_sum, weighted)
    attn_rows = (
        (weighted / running_sum[..., None])
        .transpose(2, 0, 1, 3)
        .reshape(rows_here, q_heads * HEAD_SIZE)
        .astype(jnp.bfloat16)
    )
    head_terms = jnp.dot(
        attn_rows,
        lax.all_gather(out_weight, "expert", axis=1, tiled=True),
        preferred_element_type=jnp.float32,
    )
    width = x_rows.shape[2]
    half_width = width // tensor_count
    share_sum = lax.psum_scatter(
        head_terms.astype(jnp.bfloat16), "tensor", scatter_dimension=1, tiled=True
    ).astype(jnp.float32)
    mixed_half = (
        lax.dynamic_slice_in_dim(x_rows[0], tensor_pos * half_width, half_width, 1).astype(
            jnp.float32
        )
        + share_sum
    )
    power = lax.psum(jnp.sum(mixed_half * mixed_half, axis=1), "tensor")
    inverse = lax.rsqrt(power / width + 1e-06)
    normed = (mixed_half * inverse[:, None] * norm_gain[None, :]).astype(jnp.bfloat16)
    seq_count = lax.axis_size("seq")
    group_count = lax.axis_size("expert")
    experts = seq_count * group_count
    capacity = max(2, 3 * rows_here * TOPK // (2 * experts))
    routed = expert_ids[0].reshape(-1)
    assigned = routed.shape[0]
    member = (routed[:, None] == jnp.arange(experts, dtype=jnp.int32)[None, :]).astype(jnp.int32)
    earlier = jnp.cumsum(member, axis=0) - member
    slot_index = jnp.sum(earlier * member, axis=1)
    target = routed * capacity + slot_index
    owner_index = (
        jnp.full((experts * capacity,), assigned, jnp.int32)
        .at[target]
        .set(jnp.arange(assigned, dtype=jnp.int32))
    )
    filled = owner_index < assigned
    source = jnp.minimum(owner_index // TOPK, rows_here - 1)
    outgoing = jnp.where(filled[:, None], normed[source], jnp.zeros((), jnp.bfloat16)).reshape(
        experts, capacity, half_width
    )
    arrived = lax.all_to_all(outgoing, ("seq", "expert"), split_axis=0, concat_axis=0, tiled=True)
    slot_count = arrived.shape[1]
    whole_rows = lax.all_gather(arrived, "tensor", axis=2, tiled=True)
    flat_rows = whole_rows.reshape(-1, whole_rows.shape[2])
    gate_act = jnp.dot(flat_rows, w_gate[0], preferred_element_type=jnp.float32)
    up_act = jnp.dot(flat_rows, w_up[0], preferred_element_type=jnp.float32)
    hidden = (jax.nn.silu(gate_act) * up_act).astype(jnp.bfloat16)
    partial_value = jnp.dot(hidden, w_down[0], preferred_element_type=jnp.float32).reshape(
        arrived.shape[0], slot_count, whole_rows.shape[2]
    )
    returned = lax.all_to_all(
        lax.psum_scatter(
            partial_value.astype(jnp.bfloat16), "tensor", scatter_dimension=2, tiled=True
        ),
        ("seq", "expert"),
        split_axis=0,
        concat_axis=0,
        tiled=True,
    )
    came_back = returned.reshape(experts * capacity, half_width)
    picked = came_back[target].astype(jnp.float32)
    weights_flat = gate_weights[0].reshape(-1)
    blended = jnp.sum((picked * weights_flat[:, None]).reshape(rows_here, TOPK, half_width), axis=1)
    return (mixed_half + blended).astype(jnp.bfloat16)[None]


def solution(mesh):
    return jax.shard_map(
        per_device,
        mesh=mesh,
        in_specs=(
            P("expert", "seq", "tensor"),
            P("expert", "seq", "tensor"),
            P("expert", "seq", "tensor"),
            P("expert", "seq", None),
            P("tensor", "expert"),
            P("tensor"),
            P(("seq", "expert"), None, "tensor"),
            P(("seq", "expert"), None, "tensor"),
            P(("seq", "expert"), "tensor", None),
            P("expert", "seq", None),
            P("expert", "seq", None),
        ),
        out_specs=P("expert", "seq", "tensor"),
        check_vma=False,
    )
```

profile of v0, /device:TPU:0, one launch (start us, length us, event | category | flops | bytes accessed | tf_op | source)
XLA Modules:
  0.0 479.6 jit_solution(12763142694707594264)
XLA Ops:
  6.6 0.7 all-gather.3.cloned.1.call-update
  7.3 0.8 copy.24
  8.3 1.1 copy.34
  9.6 9.7 %all_gather.13 = bf16[1,512,256]{2,1,0:T(8,128)(2,1)S(1)} all-gather(bf16[1,128,256]{2,1,0:T(8,128)(2,1)S(1)} %copy-done.3), channel_id=1, replica_groups=mesh['seq'=4,'expert'=4,'tensor'=2] {'seq'}, dimensions={1}, use_global_device_ids=true | all-gather | bytes 327680 | tf_op jit(solution)/shard_map/all_gather | solution.py:36
  19.3 0.1 copy.21
  19.5 4.5 reduce-window.6
  24.1 0.1 copy.26
  24.5 8.2 %all_gather.12 = bf16[1,512,256]{1,2,0:T(8,128)(2,1)S(1)} all-gather(bf16[1,128,256]{1,2,0:T(8,128)(2,1)S(1)} %copy.18), channel_id=1, replica_groups=mesh['seq'=4,'expert'=4,'tensor'=2] {'seq'}, dimensions={1}, use_global_device_ids=true | all-gather | bytes 327680 | tf_op jit(solution)/shard_map/all_gather | solution.py:35
  32.8 0.9 fusion.1
  33.7 1.0 fusion.2
  34.7 1.2 divide_convert_fusion
  35.9 63.4 %all-gather.3.cloned.1.call-done = bf16[2048,2048]{1,0:T(8,128)(2,1)} async-done(((bf16[2048,512]{1,0:T(8,128)(2,1)}), bf16[2048,2048]{1,0:T(8,128)(2,1)}) %all-gather.3.cloned.1.call-update) | async-done | bytes 8388624 | tf_op jit(solution)/shard_map/all_gather | solution.py:67
  99.3 5.6 %convolution_convert_fusion.1 = bf16[128,2048]{1,0:T(8,128)(2,1)} fusion(bf16[128,2048]{0,1:T(8,128)(2,1)S(1)} %bitcast.89, bf16[2048,2048]{1,0:T(8,128)(2,1)} %all-gather.3.cloned.1.call-done), kind=kOutput, calls=%fused_computation.14 | convolution fusion | flops 1074003968 | bytes 9437184 | tf_op jit(solution)/shard_map/dot_general | solution.py:65
  105.1 4.3 scatter_custom_fusion
  109.5 10.1 %reduce-scatter.3.cloned.1.call-done = bf16[128,1024]{1,0:T(8,128)(2,1)} async-done(((bf16[128,2048]{1,0:T(8,128)(2,1)}), bf16[128,1024]{1,0:T(8,128)(2,1)}) %reduce-scatter.3.cloned.1.call-update) | async-done | bytes 262160 | tf_op jit(solution)/shard_map/reduce_scatter | solution.py:72
  119.7 1.1 multiply_reduce_fusion
  120.8 4.9 %psum.7 = f32[128]{0:T(128)S(1)} all-reduce(f32[128]{0:T(128)S(1)} %multiply_reduce_fusion), channel_id=1, replica_groups=mesh['seq'=4,'expert'=4,'tensor'=2] {'tensor'}, use_global_device_ids=true, to_apply=%region_8.9 | all-reduce | flops 128 | bytes 1024 | tf_op jit(solution)/shard_map/psum | solution.py:81
  125.7 1.1 multiply_convert_fusion
  126.8 5.8 %gather_fusion = bf16[1536,1024]{1,0:T(8,128)(2,1)} fusion(bf16[128,1024]{1,0:T(8,128)(2,1)S(1)} %multiply_convert_fusion, s32[2048]{0:T(1024)S(1)} %pad_clamp_fusion), kind=kCustom, calls=%fused_computation | custom fusion | bytes 6297600 | tf_op jit(solution)/shard_map/gather | solution.py:101
  132.6 2.1 broadcast_select_fusion
  134.7 77.7 %all_to_all.10 = bf16[16,96,1024]{2,1,0:T(8,128)(2,1)} all-to-all(bf16[16,96,1024]{2,1,0:T(8,128)(2,1)S(1)} %broadcast_select_fusion), channel_id=1, replica_groups=mesh['seq'=4,'expert'=4,'tensor'=2] {'seq','expert'}, dimensions={0} | all-to-all | bytes 6291456 | tf_op jit(solution)/shard_map/all_to_all | solution.py:104
  212.5 0.2 reduce-scatter.5.cloned.1.call-start
  212.7 77.5 %all-gather.5.cloned.1.call-done = bf16[16,96,2048]{2,1,0:T(8,128)(2,1)} async-done(((bf16[16,96,1024]{2,1,0:T(8,128)(2,1)}), bf16[16,96,2048]{2,1,0:T(8,128)(2,1)}) %all-gather.5.cloned.1.call-update) | async-done | bytes 6291472 | tf_op jit(solution)/shard_map/all_gather | solution.py:106
  290.3 6.1 %fusion.10 = f32[1536,384]{1,0:T(8,128)S(1)} fusion(bf16[1536,2048]{1,0:T(8,128)(2,1)} %bitcast.100, bf16[1,2048,384]{2,1,0:T(8,128)(2,1)} %param.17), kind=kOutput, calls=%fused_computation.19 | convolution fusion | flops 2415919104 | bytes 10223616 | tf_op jit(solution)/shard_map/dot_general | solution.py:108
  296.4 3.9 fusion.4
  300.3 5.4 %convolution_convert_fusion = bf16[16,96,2048]{2,1,0:T(8,128)(2,1)} fusion(bf16[16,96,384]{2,1,0:T(8,128)(2,1)S(1)} %bitcast.102, bf16[1,384,2048]{2,1,0:T(8,128)(2,1)S(1)} %copy-done), kind=kOutput, calls=%fused_computation.3 | convolution fusion | flops 2419064832 | bytes 9043968 | tf_op jit(solution)/shard_map/dot_general | solution.py:111
  305.7 77.3 %reduce-scatter.5.cloned.1.call-done = bf16[16,96,1024]{2,1,0:T(8,128)(2,1)} async-done(((bf16[16,96,2048]{2,1,0:T(8,128)(2,1)}), bf16[16,96,1024]{2,1,0:T(8,128)(2,1)}) %reduce-scatter.5.cloned.1.call-update) | async-done | bytes 3145744 | tf_op jit(solution)/shard_map/reduce_scatter | solution.py:115
  383.0 5.6 %all-to-all-start.1 = ((bf16[16,96,1024]{2,1,0:T(8,128)(2,1)}), bf16[16,96,1024]{2,1,0:T(8,128)(2,1)}, u32[]{:S(2)}, u32[]{:S(2)}) async-start(bf16[16,96,1024]{2,1,0:T(8,128)(2,1)} %reduce-scatter.5.cloned.1.call-done), calls=%async_computation.3 | async-start | bytes 6291456 | tf_op jit(solution)/shard_map/all_to_all | solution.py:114
  388.8 72.2 %all-to-all-done.1 = bf16[16,96,1024]{2,1,0:T(8,128)(2,1)} async-done(((bf16[16,96,1024]{2,1,0:T(8,128)(2,1)}), bf16[16,96,1024]{2,1,0:T(8,128)(2,1)}, u32[]{:S(2)}, u32[]{:S(2)}) %all-to-all-start.1) | async-done | bytes 3145760 | tf_op jit(solution)/shard_map/all_to_all | solution.py:114
  460.9 8.4 %gather_fusion.1 = bf16[1024,1024]{1,0:T(8,128)(2,1)} fusion(bf16[1536,1024]{1,0:T(8,128)(2,1)} %bitcast.21, s32[1024]{0:T(1024)S(1)} %broadcast_clamp_fusion), kind=kCustom, calls=%fused_computation.1 | custom fusion | bytes 4198400 | tf_op jit(solution)/shard_map/gather | solution.py:124
  469.3 2.9 fusion
  472.3 0.8 fusion.19
  (51 shorter events, 1.3 us)
Async XLA Ops:
  6.5 293.7 %copy-start = (bf16[1,384,2048]{2,1,0:T(8,128)(2,1)S(1)}, bf16[1,384,2048]{2,1,0:T(8,128)(2,1)}, u32[]{:S(2)}) copy-start(bf16[1,384,2048]{2,1,0:T(8,128)(2,1)} %param.19) | copy-start | bytes 4718596
  6.5 17.8 %copy-start.5 = (s32[1,128,8]{1,2,0:T(8,128)S(1)}, s32[1,128,8]{1,2,0:T(8,128)}, u32[]{:S(2)}) copy-start(s32[1,128,8]{1,2,0:T(8,128)} %param.20) | copy-start | bytes 12292
  6.5 2.9 copy-start.4
  6.5 3.0 copy-start.3
  6.5 92.7 %all-gather.3.cloned.1.call-start = ((), (), s32[]{:S(2)}) async-start(), calls=%async_computation.4 | async-start | bytes 10485760 | tf_op jit(solution)/shard_map/all_gather | solution.py:67
  7.3 112.4 %reduce-scatter.3.cloned.1.call-start = ((), (), s32[]{:S(2)}) async-start(), calls=%async_computation.5 | async-start | bytes 786432 | tf_op jit(solution)/shard_map/reduce_scatter | solution.py:72
  99.3 20.4 %copy-start.2 = (bf16[1,128,2048]{2,1,0:T(8,128)(2,1)S(1)}, bf16[1,128,2048]{2,1,0:T(8,128)(2,1)}, u32[]{:S(2)}) copy-start(bf16[1,128,2048]{2,1,0:T(8,128)(2,1)} %param.14) | copy-start | bytes 1572868
  99.3 26.4 %copy-start.6 = (f32[1024]{0:T(1024)S(1)}, f32[1024]{0:T(1024)}, u32[]{:S(2)}) copy-start(f32[1024]{0:T(1024)} %param.16) | copy-start | bytes 12292
  104.9 185.4 %all-gather.5.cloned.1.call-start = ((), (), s32[]{:S(2)}) async-start(), calls=%async_computation.6 | async-start | bytes 9437184 | tf_op jit(solution)/shard_map/all_gather | solution.py:106
  212.5 170.5 %reduce-scatter.5.cloned.1.call-start = ((), (), s32[]{:S(2)}) async-start(), calls=%async_computation.7 | async-start | bytes 9437184 | tf_op jit(solution)/shard_map/reduce_scatter | solution.py:115
  290.3 6.1 %copy-start.8 = (bf16[16,96,2048]{2,1,0:T(8,128)(2,1)S(1)}, bf16[16,96,2048]{2,1,0:T(8,128)(2,1)}, u32[]{:S(2)}) copy-start(bf16[16,96,2048]{2,1,0:T(8,128)(2,1)} %all-gather.5.cloned.1.call-done) | copy-start | bytes 18874372
  290.3 6.1 %copy-start.9 = (bf16[1,2048,384]{2,1,0:T(8,128)(2,1)S(1)}, bf16[1,2048,384]{2,1,0:T(8,128)(2,1)}, u32[]{:S(2)}) copy-start(bf16[1,2048,384]{2,1,0:T(8,128)(2,1)} %param.18) | copy-start | bytes 4718596
  305.7 83.0 %copy-start.7 = (f32[1,128,8]{1,2,0:T(8,128)S(1)}, f32[1,128,8]{1,2,0:T(8,128)}, u32[]{:S(2)}) copy-start(f32[1,128,8]{1,2,0:T(8,128)} %param.21) | copy-start | bytes 12292
  383.0 77.9 %all-to-all-start.1 = ((bf16[16,96,1024]{2,1,0:T(8,128)(2,1)}), bf16[16,96,1024]{2,1,0:T(8,128)(2,1)}, u32[]{:S(2)}, u32[]{:S(2)}) async-start(bf16[16,96,1024]{2,1,0:T(8,128)(2,1)} %reduce-scatter.5.cloned.1.call-done), calls=%async_computation.3 | async-start | bytes 6291456 | tf_op jit(solution)/shard_map/all_to_all | solution.py:114
  460.9 11.3 %copy-start.1 = (bf16[128,1024]{1,0:T(8,128)(2,1)S(1)}, bf16[128,1024]{1,0:T(8,128)(2,1)}, u32[]{:S(2)}) copy-start(bf16[128,1024]{1,0:T(8,128)(2,1)} %reduce-scatter.3.cloned.1.call-done) | copy-start | bytes 786436
Sparse Core Ops, SparseCore 0:
  9.2 90.0 all-gather.2
  105.0 14.6 reduce-scatter.2
  212.6 77.5 all-gather.4
  305.8 77.1 reduce-scatter.4
where the time goes:
time: 480 us
  waiting for transfers between devices  301 us (63%)
  blocking collectives  101 us (21%)
  matrix products  23 us (5%)
  local copies, waits for them, and re-layouts  21.6 us (4%)
  other arithmetic  13.8 us (3%)
  between operations  13.4 us (3%)
  starting transfers between devices  5.98 us (1%)
    all_to_all x1, blocking collectives, per_device(): lax.all_to_all(outgoing, ('seq', 'expert'), split_axis=0, concat_axis=0,...  77.7 us
    all_gather x1, waiting for transfers between devices, per_device(): whole_rows = lax.all_gather(arrived, 'tensor', axis=2, tiled=True)  77.5 us
    reduce_scatter x1, waiting for transfers between devices, per_device(): lax.psum_scatter(partial_value.astype(jnp.bfloat16), 'tensor', scatter_di...  77.3 us
    all_to_all x1, waiting for transfers between devices, per_device(): lax.all_to_all(lax.psum_scatter(partial_value.astype(jnp.bfloat16), 'tens...  72.2 us
    all_gather x1, waiting for transfers between devices, per_device(): lax.all_gather(out_weight, 'expert', axis=1, tiled=True)  63.4 us
    reduce_scatter x1, waiting for transfers between devices, per_device(): lax.psum_scatter(head_terms.astype(jnp.bfloat16), 'tensor', scatter_dimen...  10.1 us
    all_gather x1, blocking collectives, per_device(): lax.all_gather(value_rows, 'seq', axis=1, tiled=True)  9.72 us
  transfers between devices with their start and end apart: 5, of which 5 were waited for; matrix products, arithmetic and copies ran while one was open for 3% of the time, Pallas kernels for 0%

commit v1 on v0

--- a/solution.py
+++ b/solution.py
@@ -6,6 +6,27 @@
 
 HEAD_SIZE = 128
 TOPK = 8
+
+
+def ring_gather(value, axis, dim):
+    size, index, rows = (lax.axis_size(axis), lax.axis_index(axis), value.shape[dim])
+    upward = [(i, (i + 1) % size) for i in range(size)]
+    downward = [(i, (i - 1) % size) for i in range(size)]
+    out = jnp.zeros((*value.shape[:dim], size * rows, *value.shape[dim + 1 :]), value.dtype)
+    out = lax.dynamic_update_slice_in_dim(out, value, index * rows, axis=dim)
+    from_left = from_right = value
+    half = size // 2
+    for turn in range(1, half + 1):
+        from_left = lax.ppermute(from_left, axis, upward)
+        out = lax.dynamic_update_slice_in_dim(
+            out, from_left, (index - turn) % size * rows, axis=dim
+        )
+        if turn < size - half:
+            from_right = lax.ppermute(from_right, axis, downward)
+            out = lax.dynamic_update_slice_in_dim(
+                out, from_right, (index + turn) % size * rows, axis=dim
+            )
+    return out
 
 
 def per_device(
@@ -63,9 +84,7 @@
         .astype(jnp.bfloat16)
     )
     head_terms = jnp.dot(
-        attn_rows,
-        lax.all_gather(out_weight, "expert", axis=1, tiled=True),
-        preferred_element_type=jnp.float32,
+        attn_rows, ring_gather(out_weight, "expert", 1), preferred_element_type=jnp.float32
     )
     width = x_rows.shape[2]
     half_width = width // tensor_count

time: 480 us -> 526 us (1.096)
  waiting for transfers between devices: 301 us -> 335 us
  local copies, waits for them, and re-layouts: 21.6 us -> 31.3 us
    ppermute x0 -> x3, waiting for transfers between devices: none -> 97.4 us  [the longest x2 74.4 us: ring_gather(): from_left = lax.ppermute(from_left, axis, upward)]
    all_gather x1 -> x0, waiting for transfers between devices: 63.4 us -> none  [per_device(): lax.all_gather(out_weight, 'expert', axis=1, tiled=True)]
    dynamic_update_slice x0 -> x4, local copies, waits for them, and re-layouts: none -> 6.06 us  [the longest x2 3.82 us: ring_gather(): lax.dynamic_update_slice_in_dim(out, from_left, (index - turn) % size * r...]
  transfers between devices with their start and end apart: 5 -> 7, of which waited for: 5 -> 7; matrix products, arithmetic and copies ran while one was open for 3% -> 4% of each run, Pallas kernels for 0% -> 0%
where the time goes in v1:
time: 526 us
  waiting for transfers between devices  335 us (64%)
  blocking collectives  99.6 us (19%)
  local copies, waits for them, and re-layouts  31.3 us (6%)
  matrix products  21.5 us (4%)
  other arithmetic  13.8 us (3%)
  between operations  13.4 us (3%)
  starting transfers between devices  11 us (2%)
    all_to_all x1, blocking collectives, per_device(): lax.all_to_all(outgoing, ('seq', 'expert'), split_axis=0, concat_axis=0,...  77.8 us
    all_gather x1, waiting for transfers between devices, per_device(): whole_rows = lax.all_gather(arrived, 'tensor', axis=2, tiled=True)  77.5 us
    reduce_scatter x1, waiting for transfers between devices, per_device(): lax.psum_scatter(partial_value.astype(jnp.bfloat16), 'tensor', scatter_di...  77.3 us
    ppermute x2, waiting for transfers between devices, ring_gather(): from_left = lax.ppermute(from_left, axis, upward)  74.4 us
    all_to_all x1, waiting for transfers between devices, per_device(): lax.all_to_all(lax.psum_scatter(partial_value.astype(jnp.bfloat16), 'tens...  72.2 us
    ppermute x1, waiting for transfers between devices, ring_gather(): from_right = lax.ppermute(from_right, axis, downward)  23 us
    reduce_scatter x1, waiting for transfers between devices, per_device(): lax.psum_scatter(head_terms.astype(jnp.bfloat16), 'tensor', scatter_dimen...  10.7 us
  transfers between devices with their start and end apart: 7, of which 7 were waited for; matrix products, arithmetic and copies ran while one was open for 4% of the time, Pallas kernels for 0%

profile of v1, /device:TPU:0, one launch (start us, length us, event | category | flops | bytes accessed | tf_op | source)
XLA Modules:
  0.0 525.7 jit_solution(17453498298412844224)
XLA Ops:
  6.5 3.0 collective-permute-start
  10.6 1.1 copy.34
  12.7 8.7 %all_gather.9 = bf16[1,512,256]{1,2,0:T(8,128)(2,1)S(1)} all-gather(bf16[1,128,256]{1,2,0:T(8,128)(2,1)S(1)} %copy.18), channel_id=1, replica_groups=mesh['seq'=4,'expert'=4,'tensor'=2] {'seq'}, dimensions={1}, use_global_device_ids=true | all-gather | bytes 327680 | tf_op jit(solution)/shard_map/all_gather | solution.py:56
  21.4 2.8 fusion.1
  24.5 32.8 %collective-permute-done = bf16[2048,512]{1,0:T(8,128)(2,1)} collective-permute-done((bf16[2048,512]{1,0:T(8,128)(2,1)}, bf16[2048,512]{1,0:T(8,128)(2,1)}, u32[]{:S(2)}, u32[]{:S(2)}) %collective-permute-start) | collective-permute-done | bytes 2097184 | tf_op jit(solution)/shard_map/ppermute | solution.py:20
  58.4 8.2 %all_gather.10 = bf16[1,512,256]{2,1,0:T(8,128)(2,1)S(1)} all-gather(bf16[1,128,256]{2,1,0:T(8,128)(2,1)S(1)} %copy-done.5), channel_id=1, replica_groups=mesh['seq'=4,'expert'=4,'tensor'=2] {'seq'}, dimensions={1}, use_global_device_ids=true | all-gather | bytes 327680 | tf_op jit(solution)/shard_map/all_gather | solution.py:57
  66.8 4.5 reduce-window.6
  73.8 1.8 copy-done.1
  76.7 1.2 divide_convert_fusion
  77.9 1.9 constant_dynamic-update-slice_fusion.2
  79.8 23.0 %collective-permute-done.1 = bf16[2048,512]{1,0:T(8,128)(2,1)} collective-permute-done((bf16[2048,512]{1,0:T(8,128)(2,1)}, bf16[2048,512]{1,0:T(8,128)(2,1)}, u32[]{:S(2)}, u32[]{:S(2)}) %collective-permute-start.1) | collective-permute-done | bytes 2097184 | tf_op jit(solution)/shard_map/ppermute | solution.py:25
  102.8 1.9 constant_dynamic-update-slice_fusion.1
  104.7 41.6 %collective-permute-done.2 = bf16[2048,512]{1,0:T(8,128)(2,1)} collective-permute-done((bf16[2048,512]{1,0:T(8,128)(2,1)}, bf16[2048,512]{1,0:T(8,128)(2,1)}, u32[]{:S(2)}, u32[]{:S(2)}) %collective-permute-start.2) | collective-permute-done | bytes 2097184 | tf_op jit(solution)/shard_map/ppermute | solution.py:20
  146.4 1.9 constant_dynamic-update-slice_fusion
  148.3 2.1 convolution_convert_fusion.1
  150.6 4.3 scatter_custom_fusion
  155.1 10.7 %reduce-scatter.3.cloned.1.call-done = bf16[128,1024]{1,0:T(8,128)(2,1)} async-done(((bf16[128,2048]{1,0:T(8,128)(2,1)}), bf16[128,1024]{1,0:T(8,128)(2,1)}) %reduce-scatter.3.cloned.1.call-update) | async-done | bytes 262160 | tf_op jit(solution)/shard_map/reduce_scatter | solution.py:91
  165.8 1.1 multiply_reduce_fusion
  166.9 4.9 psum.7
  171.8 1.1 multiply_convert_fusion
  172.9 5.8 %gather_fusion = bf16[1536,1024]{1,0:T(8,128)(2,1)} fusion(bf16[128,1024]{1,0:T(8,128)(2,1)S(1)} %multiply_convert_fusion, s32[2048]{0:T(1024)S(1)} %pad_clamp_fusion), kind=kCustom, calls=%fused_computation | custom fusion | bytes 6297600 | tf_op jit(solution)/shard_map/gather | solution.py:120
  178.7 2.1 broadcast_select_fusion
  180.8 77.8 %all_to_all.10 = bf16[16,96,1024]{2,1,0:T(8,128)(2,1)} all-to-all(bf16[16,96,1024]{2,1,0:T(8,128)(2,1)S(1)} %broadcast_select_fusion), channel_id=1, replica_groups=mesh['seq'=4,'expert'=4,'tensor'=2] {'seq','expert'}, dimensions={0} | all-to-all | bytes 6291456 | tf_op jit(solution)/shard_map/all_to_all | solution.py:123
  258.8 77.5 %all-gather.2.cloned.1.call-done = bf16[16,96,2048]{2,1,0:T(8,128)(2,1)} async-done(((bf16[16,96,1024]{2,1,0:T(8,128)(2,1)}), bf16[16,96,2048]{2,1,0:T(8,128)(2,1)}) %all-gather.2.cloned.1.call-update) | async-done | bytes 6291472 | tf_op jit(solution)/shard_map/all_gather | solution.py:125
  336.3 6.1 %fusion.10 = f32[1536,384]{1,0:T(8,128)S(1)} fusion(bf16[1536,2048]{1,0:T(8,128)(2,1)} %bitcast.100, bf16[1,2048,384]{2,1,0:T(8,128)(2,1)} %param.17), kind=kOutput, calls=%fused_computation.19 | convolution fusion | flops 2415919104 | bytes 10223616 | tf_op jit(solution)/shard_map/dot_general | solution.py:127
  342.5 3.9 fusion.4
  346.4 5.4 %convolution_convert_fusion = bf16[16,96,2048]{2,1,0:T(8,128)(2,1)} fusion(bf16[16,96,384]{2,1,0:T(8,128)(2,1)S(1)} %bitcast.102, bf16[1,384,2048]{2,1,0:T(8,128)(2,1)S(1)} %copy-done), kind=kOutput, calls=%fused_computation.3 | convolution fusion | flops 2419064832 | bytes 9043968 | tf_op jit(solution)/shard_map/dot_general | solution.py:130
  351.8 77.3 %reduce-scatter.5.cloned.1.call-done = bf16[16,96,1024]{2,1,0:T(8,128)(2,1)} async-done(((bf16[16,96,2048]{2,1,0:T(8,128)(2,1)}), bf16[16,96,1024]{2,1,0:T(8,128)(2,1)}) %reduce-scatter.5.cloned.1.call-update) | async-done | bytes 3145744 | tf_op jit(solution)/shard_map/reduce_scatter | solution.py:134
  429.1 5.6 %all-to-all-start.1 = ((bf16[16,96,1024]{2,1,0:T(8,128)(2,1)}), bf16[16,96,1024]{2,1,0:T(8,128)(2,1)}, u32[]{:S(2)}, u32[]{:S(2)}) async-start(bf16[16,96,1024]{2,1,0:T(8,128)(2,1)} %reduce-scatter.5.cloned.1.call-done), calls=%async_computation.3 | async-start | bytes 6291456 | tf_op jit(solution)/shard_map/all_to_all | solution.py:133
  434.9 72.2 %all-to-all-done.1 = bf16[16,96,1024]{2,1,0:T(8,128)(2,1)} async-done(((bf16[16,96,1024]{2,1,0:T(8,128)(2,1)}), bf16[16,96,1024]{2,1,0:T(8,128)(2,1)}, u32[]{:S(2)}, u32[]{:S(2)}) %all-to-all-start.1) | async-done | bytes 3145760 | tf_op jit(solution)/shard_map/all_to_all | solution.py:133
  507.0 8.4 %gather_fusion.1 = bf16[1024,1024]{1,0:T(8,128)(2,1)} fusion(bf16[1536,1024]{1,0:T(8,128)(2,1)} %bitcast.21, s32[1024]{0:T(1024)S(1)} %broadcast_clamp_fusion), kind=kCustom, calls=%fused_computation.1 | custom fusion | bytes 4198400 | tf_op jit(solution)/shard_map/gather | solution.py:143
  515.4 2.9 fusion
  (61 shorter events, 8.5 us)
Async XLA Ops:
  6.5 339.8 %copy-start = (bf16[1,384,2048]{2,1,0:T(8,128)(2,1)S(1)}, bf16[1,384,2048]{2,1,0:T(8,128)(2,1)}, u32[]{:S(2)}) copy-start(bf16[1,384,2048]{2,1,0:T(8,128)(2,1)} %param.19) | copy-start | bytes 4718596
  6.5 17.7 %copy-start.6 = (s32[1,128,8]{1,2,0:T(8,128)S(1)}, s32[1,128,8]{1,2,0:T(8,128)}, u32[]{:S(2)}) copy-start(s32[1,128,8]{1,2,0:T(8,128)} %param.20) | copy-start | bytes 12292
  6.5 51.8 %copy-start.5 = (bf16[1,128,256]{2,1,0:T(8,128)(2,1)S(1)}, bf16[1,128,256]{2,1,0:T(8,128)(2,1)}, u32[]{:S(2)}) copy-start(bf16[1,128,256]{2,1,0:T(8,128)(2,1)} %param.13) | copy-start | bytes 196612
  6.5 159.2 %reduce-scatter.3.cloned.1.call-start = ((), (), s32[]{:S(2)}) async-start(), calls=%async_computation.4 | async-start | bytes 786432 | tf_op jit(solution)/shard_map/reduce_scatter | solution.py:91
  6.5 50.8 %collective-permute-start = (bf16[2048,512]{1,0:T(8,128)(2,1)}, bf16[2048,512]{1,0:T(8,128)(2,1)}, u32[]{:S(2)}, u32[]{:S(2)}) collective-permute-start(bf16[2048,512]{1,0:T(8,128)(2,1)} %param.15), channel_id=1, source_target_pairs={{0,2},{2,4},{4,6},{6,0},{1,3},{3,5},{5,7},{7,1},{8,10},{10,12},{12... | collective-permute-start | bytes 6291464 | tf_op jit(solution)/shard_map/ppermute | solution.py:20
  9.6 93.2 %collective-permute-start.1 = (bf16[2048,512]{1,0:T(8,128)(2,1)}, bf16[2048,512]{1,0:T(8,128)(2,1)}, u32[]{:S(2)}, u32[]{:S(2)}) collective-permute-start(bf16[2048,512]{1,0:T(8,128)(2,1)} %param.15), channel_id=1, source_target_pairs={{0,6},{2,0},{4,2},{6,4},{1,7},{3,1},{5,3},{7,5},{8,14},{10,8},{12,... | collective-permute-start | bytes 6291464 | tf_op jit(solution)/shard_map/ppermute | solution.py:25
  57.3 89.0 %collective-permute-start.2 = (bf16[2048,512]{1,0:T(8,128)(2,1)}, bf16[2048,512]{1,0:T(8,128)(2,1)}, u32[]{:S(2)}, u32[]{:S(2)}) collective-permute-start(bf16[2048,512]{1,0:T(8,128)(2,1)} %collective-permute-done), channel_id=1, source_target_pairs={{0,2},{2,4},{4,6},{6,0},{1,3},{3,5},{5,7},{7,1},{8,10},{10,12},{12... | collective-permute-start | bytes 6291464 | tf_op jit(solution)/shard_map/ppermute | solution.py:20
  71.8 1.6 copy-start.3
  73.4 2.2 copy-start.1
  148.3 17.5 %copy-start.4 = (bf16[1,128,2048]{2,1,0:T(8,128)(2,1)S(1)}, bf16[1,128,2048]{2,1,0:T(8,128)(2,1)}, u32[]{:S(2)}) copy-start(bf16[1,128,2048]{2,1,0:T(8,128)(2,1)} %param.14) | copy-start | bytes 1572868
  148.3 23.5 %copy-start.7 = (f32[1024]{0:T(1024)S(1)}, f32[1024]{0:T(1024)}, u32[]{:S(2)}) copy-start(f32[1024]{0:T(1024)} %param.16) | copy-start | bytes 12292
  150.4 185.9 %all-gather.2.cloned.1.call-start = ((), (), s32[]{:S(2)}) async-start(), calls=%async_computation.5 | async-start | bytes 9437184 | tf_op jit(solution)/shard_map/all_gather | solution.py:125
  258.6 170.5 %reduce-scatter.5.cloned.1.call-start = ((), (), s32[]{:S(2)}) async-start(), calls=%async_computation.6 | async-start | bytes 9437184 | tf_op jit(solution)/shard_map/reduce_scatter | solution.py:134
  336.3 6.1 %copy-start.9 = (bf16[16,96,2048]{2,1,0:T(8,128)(2,1)S(1)}, bf16[16,96,2048]{2,1,0:T(8,128)(2,1)}, u32[]{:S(2)}) copy-start(bf16[16,96,2048]{2,1,0:T(8,128)(2,1)} %all-gather.2.cloned.1.call-done) | copy-start | bytes 18874372
  336.3 6.1 %copy-start.10 = (bf16[1,2048,384]{2,1,0:T(8,128)(2,1)S(1)}, bf16[1,2048,384]{2,1,0:T(8,128)(2,1)}, u32[]{:S(2)}) copy-start(bf16[1,2048,384]{2,1,0:T(8,128)(2,1)} %param.18) | copy-start | bytes 4718596
  351.8 83.0 %copy-start.8 = (f32[1,128,8]{1,2,0:T(8,128)S(1)}, f32[1,128,8]{1,2,0:T(8,128)}, u32[]{:S(2)}) copy-start(f32[1,128,8]{1,2,0:T(8,128)} %param.21) | copy-start | bytes 12292
  429.1 77.9 %all-to-all-start.1 = ((bf16[16,96,1024]{2,1,0:T(8,128)(2,1)}), bf16[16,96,1024]{2,1,0:T(8,128)(2,1)}, u32[]{:S(2)}, u32[]{:S(2)}) async-start(bf16[16,96,1024]{2,1,0:T(8,128)(2,1)} %reduce-scatter.5.cloned.1.call-done), calls=%async_computation.3 | async-start | bytes 6291456 | tf_op jit(solution)/shard_map/all_to_all | solution.py:133
  507.0 11.3 %copy-start.2 = (bf16[128,1024]{1,0:T(8,128)(2,1)S(1)}, bf16[128,1024]{1,0:T(8,128)(2,1)}, u32[]{:S(2)}) copy-start(bf16[128,1024]{1,0:T(8,128)(2,1)} %reduce-scatter.3.cloned.1.call-done) | copy-start | bytes 786436
Sparse Core Ops, SparseCore 0:
  150.5 15.1 reduce-scatter.2
  258.7 77.5 all-gather.1
  351.9 77.1 reduce-scatter.4
